TPU v7x, 256 devices: a whole 4x4x8 slice. The times are simulated.
256 devices in a mesh: col: 64 (over z, x, core), rhs: 4 (over y).
Axes of the slice: x: 4, y: 4, z: 8, core: 2. Of those that a mesh axis runs over, the one named last changes fastest.
Arguments:
- rhs_block: bfloat16 [16384, 4096], P('col', 'rhs'), may hold values from -6 to 6
- solution: bfloat16 [196608, 4096], P('col', 'rhs'), may hold values from -6 to 6
- factor: bfloat16 [64, 6, 256, 3072], P('col', None, 'rhs'), may hold values from -0.109375 to 0.109375
- tile_list: int32 [64, 6], P('col'), may hold values 0 or 1
- diag_inverse: bfloat16 [64, 256, 256], P('col'), may hold values from -0.375 to 0.375
Outputs:
- solved_rows: bfloat16 [16384, 4096], P('col', 'rhs')
All inputs are finite; a program needn't handle non-finite values. No bound on the sum of `tile_list` on one device may be relied on, other than what follows from the above.
Results may differ from a plain program's by a relative error of at most 0.0049.
Values may be sent and summed in bfloat16 or wider, within the bound.
A program may use at most 64 MiB of HBM per device.

v0:
```python
import jax
import jax.numpy as jnp
from jax import lax
from jax.sharding import PartitionSpec as P


def from_behind(block, axis, distance):
    devices = range(lax.axis_size(axis))
    route = [((i - distance) % len(devices), i) for i in devices]
    return lax.ppermute(block, axis, route)


def per_device(rhs_block, solution, factor, tile_list, diag_inverse):
    hop_count = factor.shape[1]
    carried = jnp.zeros((rhs_block.shape[0], rhs_block.shape[1]), jnp.float32)
    for offset in reversed(range(hop_count)):
        product_term = jnp.dot(
            lax.all_gather(factor[0, offset], "rhs", axis=0, tiled=True),
            solution,
            preferred_element_type=jnp.float32,
        )
        carried = carried + product_term * tile_list[0, offset].astype(jnp.float32)
        carried = from_behind(carried, "col", 1)
    remaining = (rhs_block.astype(jnp.float32) - carried).astype(jnp.bfloat16)
    return jnp.dot(diag_inverse[0], remaining, preferred_element_type=jnp.float32).astype(
        jnp.bfloat16
    )


def solution(mesh):
    in_specs = (
        P("col", "rhs"),
        P("col", "rhs"),
        P("col", None, "rhs", None),
        P("col", None),
        P("col", None, None),
    )
    out_specs = P("col", "rhs")
    return jax.shard_map(
        per_device, mesh=mesh, in_specs=in_specs, out_specs=out_specs, check_vma=False
    )
```

profile of v0, /device:TPU:8, one launch (start us, length us, event | category | flops | bytes accessed | tf_op | source)
XLA Modules:
  0.0 225.7 jit_solution(13746546917414927949)
XLA Ops:
  6.5 3.0 %fusion.35 = (bf16[1,1,64,3072]{3,2,1,0:T(8,128)(2,1)}, bf16[1,1,64,3072]{3,2,1,0:T(8,128)(2,1)}, bf16[1,1,64,3072]{3,2,1,0:T(8,128)(2,1)}, bf16[1,1,64,3072]{3,...) fusion(bf16[1,6,64,3072]{3,2,1,0:T(8,128)(2,1)} %param.7), kind=kLoop, calls=%fused_computation.23 | loop fusion | bytes 4718592 | tf_op jit(solution)/shard_map/slice | solution.py:18
  9.7 0.7 all-gather.15.cloned.1.call-update
  10.4 0.7 all-gather.17.cloned.1.call-update
  11.1 0.5 all-gather.19.cloned.1.call-update
  11.7 0.7 fusion.36
  13.0 27.7 %all-gather.13.cloned.1.call-done = bf16[1,1,256,3072]{3,2,1,0:T(8,128)(2,1)} async-done(((bf16[1,1,64,3072]{3,2,1,0:T(8,128)(2,1)}), bf16[1,1,256,3072]{3,2,1,0:T(8,128)(2,1)}) %all-gather.13.cloned.1.call-update) | async-done | bytes 1572880 | tf_op jit(solution)/shard_map/all_gather | solution.py:18
  40.7 5.1 %fusion.12 = f32[256,1024]{1,0:T(8,128)S(1)} fusion(bf16[3072,1024]{1,0:T(8,128)(2,1)} %param.6, bf16[1,1,256,3072]{3,2,1,0:T(8,128)(2,1)} %all-gather.13.cloned.1.call-done, f32[]{:T(128)} %bitcast.1), kind=kOutput, calls=%fused_computation.12 | convolution fusion | flops 1610874880 | bytes 8912900 | tf_op jit(solution)/shard_map/dot_general | solution.py:17
  46.5 25.1 %all-gather.15.cloned.1.call-done = bf16[1,1,256,3072]{3,2,1,0:T(8,128)(2,1)} async-done(((bf16[1,1,64,3072]{3,2,1,0:T(8,128)(2,1)}), bf16[1,1,256,3072]{3,2,1,0:T(8,128)(2,1)}) %all-gather.15.cloned.1.call-update) | async-done | bytes 1572880 | tf_op jit(solution)/shard_map/all_gather | solution.py:18
  71.5 5.1 %fusion.30 = f32[256,1024]{1,0:T(8,128)S(1)} fusion(f32[256,1024]{1,0:T(8,128)S(1)} %collective-permute-done, bf16[3072,1024]{1,0:T(8,128)(2,1)} %param.6, bf16[1,1,256,3072]{3,2,1,0:T(8,128)(2,1)} %all-gather.15.cloned.1.call-done, f32[]{:T(128)} %bitcast.3), kind=kOutput, calls=%fused_computation.18 | convolution fusion | flops 1611137024 | bytes 9961476 | tf_op jit(solution)/shard_map/dot_general | solution.py:17
  77.3 25.1 %all-gather.17.cloned.1.call-done = bf16[1,1,256,3072]{3,2,1,0:T(8,128)(2,1)} async-done(((bf16[1,1,64,3072]{3,2,1,0:T(8,128)(2,1)}), bf16[1,1,256,3072]{3,2,1,0:T(8,128)(2,1)}) %all-gather.17.cloned.1.call-update) | async-done | bytes 1572880 | tf_op jit(solution)/shard_map/all_gather | solution.py:18
  102.4 5.1 %fusion.18 = f32[256,1024]{1,0:T(8,128)S(1)} fusion(bf16[3072,1024]{1,0:T(8,128)(2,1)} %param.6, bf16[1,1,256,3072]{3,2,1,0:T(8,128)(2,1)} %all-gather.17.cloned.1.call-done, f32[]{:T(128)} %bitcast.5), kind=kOutput, calls=%fused_computation.14 | convolution fusion | flops 1610874880 | bytes 8912900 | tf_op jit(solution)/shard_map/dot_general | solution.py:17
  107.5 0.2 add.16
  108.3 24.8 %all-gather.19.cloned.1.call-done = bf16[1,1,256,3072]{3,2,1,0:T(8,128)(2,1)} async-done(((bf16[1,1,64,3072]{3,2,1,0:T(8,128)(2,1)}), bf16[1,1,256,3072]{3,2,1,0:T(8,128)(2,1)}) %all-gather.19.cloned.1.call-update) | async-done | bytes 1572880 | tf_op jit(solution)/shard_map/all_gather | solution.py:18
  133.1 5.1 %fusion.21 = f32[256,1024]{1,0:T(8,128)S(1)} fusion(bf16[3072,1024]{1,0:T(8,128)(2,1)} %param.6, bf16[1,1,256,3072]{3,2,1,0:T(8,128)(2,1)} %all-gather.19.cloned.1.call-done, f32[]{:T(128)} %bitcast.7), kind=kOutput, calls=%fused_computation.15 | convolution fusion | flops 1610874880 | bytes 8912900 | tf_op jit(solution)/shard_map/dot_general | solution.py:17
  138.2 0.2 add.17
  139.1 24.7 %all-gather.21.cloned.1.call-done = bf16[1,1,256,3072]{3,2,1,0:T(8,128)(2,1)} async-done(((bf16[1,1,64,3072]{3,2,1,0:T(8,128)(2,1)}), bf16[1,1,256,3072]{3,2,1,0:T(8,128)(2,1)}) %all-gather.21.cloned.1.call-update) | async-done | bytes 1572880 | tf_op jit(solution)/shard_map/all_gather | solution.py:18
  163.8 5.1 %fusion.24 = f32[256,1024]{1,0:T(8,128)S(1)} fusion(bf16[3072,1024]{1,0:T(8,128)(2,1)} %param.6, bf16[1,1,256,3072]{3,2,1,0:T(8,128)(2,1)} %all-gather.21.cloned.1.call-done, f32[]{:T(128)} %bitcast.9), kind=kOutput, calls=%fused_computation.16 | convolution fusion | flops 1610874880 | bytes 8912900 | tf_op jit(solution)/shard_map/dot_general | solution.py:17
  169.1 0.3 collective-permute-start.4
  170.0 24.6 %all-gather.23.cloned.1.call-done = bf16[1,1,256,3072]{3,2,1,0:T(8,128)(2,1)} async-done(((bf16[1,1,64,3072]{3,2,1,0:T(8,128)(2,1)}), bf16[1,1,256,3072]{3,2,1,0:T(8,128)(2,1)}) %all-gather.23.cloned.1.call-update) | async-done | bytes 1572880 | tf_op jit(solution)/shard_map/all_gather | solution.py:18
  194.5 5.1 %fusion.27 = f32[256,1024]{1,0:T(8,128)S(1)} fusion(bf16[3072,1024]{1,0:T(8,128)(2,1)} %param.6, bf16[1,1,256,3072]{3,2,1,0:T(8,128)(2,1)} %all-gather.23.cloned.1.call-done, f32[]{:T(128)} %bitcast.11), kind=kOutput, calls=%fused_computation.17 | convolution fusion | flops 1610874880 | bytes 8912900 | tf_op jit(solution)/shard_map/dot_general | solution.py:17
  199.6 0.2 add.19
  199.9 17.5 %collective-permute-done.5 = f32[256,1024]{1,0:T(8,128)S(1)} collective-permute-done((f32[256,1024]{1,0:T(8,128)S(1)}, f32[256,1024]{1,0:T(8,128)S(1)}, u32[]{:S(2)}, u32[]{:S(2)}) %collective-permute-start.5) | collective-permute-done | bytes 1048608 | tf_op jit(solution)/shard_map/ppermute | solution.py:10
  217.4 0.4 fusion.33
  217.8 1.0 copy.6
  (26 shorter events, 0.8 us)
Async XLA Ops:
  6.5 210.9 %copy-start = (bf16[1,256,256]{2,1,0:T(8,128)(2,1)S(1)}, bf16[1,256,256]{2,1,0:T(8,128)(2,1)}, u32[]{:S(2)}) copy-start(bf16[1,256,256]{2,1,0:T(8,128)(2,1)} %param.9) | copy-start | bytes 393220
  6.5 34.2 %all-gather.13.cloned.1.call-start = ((), (), s32[]{:S(2)}) async-start(), calls=%async_computation | async-start | bytes 1966080 | tf_op jit(solution)/shard_map/all_gather | solution.py:18
  9.6 2.1 copy-start.2
  9.6 61.9 %all-gather.15.cloned.1.call-start = ((), (), s32[]{:S(2)}) async-start(), calls=%async_computation.1 | async-start | bytes 1966080 | tf_op jit(solution)/shard_map/all_gather | solution.py:18
  10.4 92.0 %all-gather.17.cloned.1.call-start = ((), (), s32[]{:S(2)}) async-start(), calls=%async_computation.2 | async-start | bytes 1966080 | tf_op jit(solution)/shard_map/all_gather | solution.py:18
  11.1 122.0 %all-gather.19.cloned.1.call-start = ((), (), s32[]{:S(2)}) async-start(), calls=%async_computation.3 | async-start | bytes 1966080 | tf_op jit(solution)/shard_map/all_gather | solution.py:18
  11.7 152.2 %all-gather.21.cloned.1.call-start = ((), (), s32[]{:S(2)}) async-start(), calls=%async_computation.4 | async-start | bytes 1966080 | tf_op jit(solution)/shard_map/all_gather | solution.py:18
  45.8 25.8 %collective-permute-start = (f32[256,1024]{1,0:T(8,128)S(1)}, f32[256,1024]{1,0:T(8,128)S(1)}, u32[]{:S(2)}, u32[]{:S(2)}) collective-permute-start(f32[256,1024]{1,0:T(8,128)S(1)} %fusion.12), channel_id=1, source_target_pairs={{252,0},{0,4},{4,8},{8,12},{12,16},{16,20},{20,24},{24,28},{28,32}... | collective-permute-start | bytes 3145736 | tf_op jit(solution)/shard_map/ppermute | solution.py:10
  45.9 148.7 %all-gather.23.cloned.1.call-start = ((), (), s32[]{:S(2)}) async-start(), calls=%async_computation.5 | async-start | bytes 1966080 | tf_op jit(solution)/shard_map/all_gather | solution.py:18
  76.6 30.9 %collective-permute-start.1 = (f32[256,1024]{1,0:T(8,128)S(1)}, f32[256,1024]{1,0:T(8,128)S(1)}, u32[]{:S(2)}, u32[]{:S(2)}) collective-permute-start(f32[256,1024]{1,0:T(8,128)S(1)} %fusion.30), channel_id=1, source_target_pairs={{252,0},{0,4},{4,8},{8,12},{12,16},{16,20},{20,24},{24,28},{28,32}... | collective-permute-start | bytes 3145736 | tf_op jit(solution)/shard_map/ppermute | solution.py:10
  107.6 30.5 %collective-permute-start.2 = (f32[256,1024]{1,0:T(8,128)S(1)}, f32[256,1024]{1,0:T(8,128)S(1)}, u32[]{:S(2)}, u32[]{:S(2)}) collective-permute-start(f32[256,1024]{1,0:T(8,128)S(1)} %add.16), channel_id=1, source_target_pairs={{252,0},{0,4},{4,8},{8,12},{12,16},{16,20},{20,24},{24,28},{28,32}... | collective-permute-start | bytes 3145736 | tf_op jit(solution)/shard_map/ppermute | solution.py:10
  138.4 30.5 %collective-permute-start.3 = (f32[256,1024]{1,0:T(8,128)S(1)}, f32[256,1024]{1,0:T(8,128)S(1)}, u32[]{:S(2)}, u32[]{:S(2)}) collective-permute-start(f32[256,1024]{1,0:T(8,128)S(1)} %add.17), channel_id=1, source_target_pairs={{252,0},{0,4},{4,8},{8,12},{12,16},{16,20},{20,24},{24,28},{28,32}... | collective-permute-start | bytes 3145736 | tf_op jit(solution)/shard_map/ppermute | solution.py:10
  169.1 30.6 %collective-permute-start.4 = (f32[256,1024]{1,0:T(8,128)S(1)}, f32[256,1024]{1,0:T(8,128)S(1)}, u32[]{:S(2)}, u32[]{:S(2)}) collective-permute-start(f32[256,1024]{1,0:T(8,128)S(1)} %add.18), channel_id=1, source_target_pairs={{252,0},{0,4},{4,8},{8,12},{12,16},{16,20},{20,24},{24,28},{28,32}... | collective-permute-start | bytes 3145736 | tf_op jit(solution)/shard_map/ppermute | solution.py:10
  199.6 17.8 %copy-start.1 = (bf16[256,1024]{1,0:T(8,128)(2,1)S(1)}, bf16[256,1024]{1,0:T(8,128)(2,1)}, u32[]{:S(2)}) copy-start(bf16[256,1024]{1,0:T(8,128)(2,1)} %param.5) | copy-start | bytes 1572868
  199.8 17.6 %collective-permute-start.5 = (f32[256,1024]{1,0:T(8,128)S(1)}, f32[256,1024]{1,0:T(8,128)S(1)}, u32[]{:S(2)}, u32[]{:S(2)}) collective-permute-start(f32[256,1024]{1,0:T(8,128)S(1)} %add.19), channel_id=1, source_target_pairs={{252,0},{0,4},{4,8},{8,12},{12,16},{16,20},{20,24},{24,28},{28,32}... | collective-permute-start | bytes 3145736 | tf_op jit(solution)/shard_map/ppermute | solution.py:10
Sparse Core Ops, SparseCore 0:
  9.7 30.9 all-gather.12
  42.5 29.0 all-gather.14
  73.4 29.0 all-gather.16
  104.1 29.0 all-gather.18
  134.8 29.0 all-gather.20
  165.5 29.0 all-gather.22
where the time goes:
time: 226 us
  waiting for transfers between devices  171 us (76%)
  matrix products  30.8 us (14%)
  between operations  17.3 us (8%)
  local copies, waits for them, and re-layouts  4.73 us (2%)
    all_gather x6, waiting for transfers between devices, per_device(): lax.all_gather(factor[0, offset], 'rhs', axis=0, tiled=True)  152 us
    dot_general x6, matrix products, per_device(): jnp.dot(lax.all_gather(factor[0, offset], 'rhs', axis=0, tiled=True), sol...  30.4 us
    ppermute x6, waiting for transfers between devices, from_behind(): return lax.ppermute(block, axis, route)  17.5 us
  transfers between devices with their start and end apart: 12, of which 7 were waited for; matrix products, arithmetic and copies ran while one was open for 14% of the time, Pallas kernels for 0%

commit v1 on v0

--- a/solution.py
+++ b/solution.py
@@ -15,7 +15,10 @@
     carried = jnp.zeros((rhs_block.shape[0], rhs_block.shape[1]), jnp.float32)
     for offset in reversed(range(hop_count)):
         product_term = jnp.dot(
-            lax.all_gather(factor[0, offset], "rhs", axis=0, tiled=True),
+            jnp.concatenate(
+                lax.all_to_all(jnp.stack([factor[0, offset]] * lax.axis_size("rhs")), "rhs", 0, 0),
+                axis=0,
+            ),
             solution,
             preferred_element_type=jnp.float32,
         )

time: 226 us -> 176 us (0.78)
  waiting for transfers between devices: 171 us -> 71 us
  starting transfers between devices: 0.88 us -> 25.4 us
  blocking collectives: 0 us -> 24 us
  between operations: 17.3 us -> 3.9 us
  local copies, waits for them, and re-layouts: 4.73 us -> 13.6 us
  other arithmetic: 0.62 us -> 6.33 us
    all_gather x6 -> x0, waiting for transfers between devices: 152 us -> none  [per_device(): lax.all_gather(factor[0, offset], 'rhs', axis=0, tiled=True)]
    all_to_all x0 -> x5, waiting for transfers between devices: none -> 48.4 us  [per_device(): lax.all_to_all(jnp.stack([factor[0, offset]] * lax.axis_size('rhs')), 'rh...]
    all_to_all x0 -> x5, starting transfers between devices: none -> 25.1 us  [per_device(): lax.all_to_all(jnp.stack([factor[0, offset]] * lax.axis_size('rhs')), 'rh...]
    all_to_all x0 -> x1, blocking collectives: none -> 24 us  [per_device(): lax.all_to_all(jnp.stack([factor[0, offset]] * lax.axis_size('rhs')), 'rh...]
    another operation x0 -> x7, local copies, waits for them, and re-layouts: none -> 11.9 us  [per_device(): jnp.stack([factor[0, offset]] * lax.axis_size('rhs'))]
    add x4, other arithmetic: 0.62 us -> 6.33 us  [per_device(): carried = carried + product_term * tile_list[0, offset].astype(jnp.float32)]
    ppermute x6, waiting for transfers between devices: 17.5 us -> 22.6 us  [from_behind(): return lax.ppermute(block, axis, route)]
    slice x1 -> x0, local copies, waits for them, and re-layouts: 3.04 us -> none  [per_device(): factor[0, offset]]
  transfers between devices with their start and end apart: 12 -> 11, of which waited for: 7 -> 7; matrix products, arithmetic and copies ran while one was open for 14% -> 25% of each run, Pallas kernels for 0% -> 0%
where the time goes in v1:
time: 176 us; the launch traced here: 175 us
  waiting for transfers between devices  71 us (40%)
  matrix products  30.6 us (17%)
  starting transfers between devices  25.4 us (14%)
  blocking collectives  24 us (14%)
  local copies, waits for them, and re-layouts  13.6 us (8%)
  other arithmetic  6.33 us (4%)
  between operations  3.9 us (2%)
    all_to_all x5, waiting for transfers between devices, per_device(): lax.all_to_all(jnp.stack([factor[0, offset]] * lax.axis_size('rhs')), 'rh...  48.4 us
    dot_general x6, matrix products, per_device(): jnp.dot(jnp.concatenate(lax.all_to_all(jnp.stack([factor[0, offset]] * la...  30.2 us
    all_to_all x5, starting transfers between devices, per_device(): lax.all_to_all(jnp.stack([factor[0, offset]] * lax.axis_size('rhs')), 'rh...  25.1 us
    all_to_all x1, blocking collectives, per_device(): lax.all_to_all(jnp.stack([factor[0, offset]] * lax.axis_size('rhs')), 'rh...  24 us
    ppermute x6, waiting for transfers between devices, from_behind(): return lax.ppermute(block, axis, route)  22.6 us
    another operation x7, local copies, waits for them, and re-layouts, per_device(): jnp.stack([factor[0, offset]] * lax.axis_size('rhs'))  11.9 us
    add x4, other arithmetic, per_device(): carried = carried + product_term * tile_list[0, offset].astype(jnp.float32)  6.33 us
  transfers between devices with their start and end apart: 11, of which 7 were waited for; matrix products, arithmetic and copies ran while one was open for 25% of the time, Pallas kernels for 0%

profile of v1, /device:TPU:8, one launch (start us, length us, event | category | flops | bytes accessed | tf_op | source)
XLA Modules:
  0.0 174.8 jit_solution(14456160461273200498)
XLA Ops:
  0.0 2.8 %slice_bitcast_fusion = (bf16[64,3072]{1,0:T(8,128)(2,1)}, bf16[64,3072]{1,0:T(8,128)(2,1)}, bf16[64,3072]{1,0:T(8,128)(2,1)}, bf16[64,3072]{1,0:T(8,128)(2,1)S(...) fusion(bf16[1,6,64,3072]{3,2,1,0:T(8,128)(2,1)} %param.7), kind=kLoop, calls=%fused_computation.10 | loop fusion | bytes 4718592 | tf_op jit(solution)/shard_map/stack;squeeze | solution.py:19
  3.0 24.0 %all_to_all.30 = bf16[4,64,3072]{2,1,0:T(8,128)(2,1)S(1)} all-to-all(bf16[4,64,3072]{2,1,0:T(8,128)(2,1)S(1)} %stack.18), channel_id=1, replica_groups=mesh['col'=64,'rhs'=4] {'rhs'}, dimensions={0} | all-to-all | bytes 3145728 | tf_op jit(solution)/shard_map/all_to_all | solution.py:19
  28.3 5.1 %all-to-all-start.1 = ((bf16[4,64,3072]{2,1,0:T(8,128)(2,1)}), bf16[4,64,3072]{2,1,0:T(8,128)(2,1)S(1)}, u32[]{:S(2)}, u32[]{:S(2)}) async-start(bf16[4,64,3072]{2,1,0:T(8,128)(2,1)} %stack.19), calls=%async_computation.1 | async-start | bytes 3145728 | tf_op jit(solution)/shard_map/all_to_all | solution.py:19
  34.7 5.6 %convolution_multiply_fusion.5 = f32[256,1024]{1,0:T(8,128)} fusion(bf16[256,3072]{1,0:T(8,128)(2,1)S(1)} %bitcast.46, bf16[3072,1024]{1,0:T(8,128)(2,1)} %param.6, f32[]{:T(128)} %bitcast.2), kind=kOutput, calls=%fused_computation.5 | convolution fusion | flops 1610874880 | bytes 8912900 | tf_op jit(solution)/shard_map/dot_general | solution.py:17
  40.3 11.5 %all-to-all-done.1 = bf16[4,64,3072]{2,1,0:T(8,128)(2,1)S(1)} async-done(((bf16[4,64,3072]{2,1,0:T(8,128)(2,1)}), bf16[4,64,3072]{2,1,0:T(8,128)(2,1)S(1)}, u32[]{:S(2)}, u32[]{:S(2)}) %all-to-all-start.1) | async-done | bytes 1572896 | tf_op jit(solution)/shard_map/all_to_all | solution.py:19
  51.8 2.3 %stack.20 = bf16[4,64,3072]{2,1,0:T(8,128)(2,1)} broadcast(bf16[64,3072]{1,0:T(8,128)(2,1)} %get-tuple-element.7), dimensions={1,2} | broadcast | bytes 1966080 | tf_op jit(solution)/shard_map/stack | solution.py:19
  54.1 5.0 %all-to-all-start.2 = ((bf16[4,64,3072]{2,1,0:T(8,128)(2,1)}), bf16[4,64,3072]{2,1,0:T(8,128)(2,1)S(1)}, u32[]{:S(2)}, u32[]{:S(2)}) async-start(bf16[4,64,3072]{2,1,0:T(8,128)(2,1)} %stack.20), calls=%async_computation.2 | async-start | bytes 3145728 | tf_op jit(solution)/shard_map/all_to_all | solution.py:19
  59.7 5.8 %fusion = f32[256,1024]{1,0:T(8,128)} fusion(f32[256,1024]{1,0:T(8,128)} %collective-permute-done, bf16[256,3072]{1,0:T(8,128)(2,1)S(1)} %bitcast.41, bf16[3072,1024]{1,0:T(8,128)(2,1)} %param.6, f32[]{:T(128)} %bitcast.5), kind=kOutput, calls=%fused_computation.6 | convolution fusion | flops 1611137024 | bytes 9961476 | tf_op jit(solution)/shard_map/dot_general | solution.py:17
  65.5 11.3 %all-to-all-done.2 = bf16[4,64,3072]{2,1,0:T(8,128)(2,1)S(1)} async-done(((bf16[4,64,3072]{2,1,0:T(8,128)(2,1)}), bf16[4,64,3072]{2,1,0:T(8,128)(2,1)S(1)}, u32[]{:S(2)}, u32[]{:S(2)}) %all-to-all-start.2) | async-done | bytes 1572896 | tf_op jit(solution)/shard_map/all_to_all | solution.py:19
  76.8 2.6 %stack.21 = bf16[4,64,3072]{2,1,0:T(8,128)(2,1)} broadcast(bf16[64,3072]{1,0:T(8,128)(2,1)} %get-tuple-element.6), dimensions={1,2} | broadcast | bytes 1966080 | tf_op jit(solution)/shard_map/stack | solution.py:19
  79.4 5.0 %all-to-all-start.3 = ((bf16[4,64,3072]{2,1,0:T(8,128)(2,1)}), bf16[4,64,3072]{2,1,0:T(8,128)(2,1)S(1)}, u32[]{:S(2)}, u32[]{:S(2)}) async-start(bf16[4,64,3072]{2,1,0:T(8,128)(2,1)} %stack.21), calls=%async_computation.3 | async-start | bytes 3145728 | tf_op jit(solution)/shard_map/all_to_all | solution.py:19
  85.0 5.1 %convolution_multiply_fusion.3 = f32[256,1024]{1,0:T(8,128)S(1)} fusion(bf16[256,3072]{1,0:T(8,128)(2,1)} %bitcast.44, bf16[3072,1024]{1,0:T(8,128)(2,1)} %param.6, f32[]{:T(128)} %bitcast.8), kind=kOutput, calls=%fused_computation.3 | convolution fusion | flops 1610874880 | bytes 8912900 | tf_op jit(solution)/shard_map/dot_general | solution.py:17
  91.2 9.9 %all-to-all-done.3 = bf16[4,64,3072]{2,1,0:T(8,128)(2,1)S(1)} async-done(((bf16[4,64,3072]{2,1,0:T(8,128)(2,1)}), bf16[4,64,3072]{2,1,0:T(8,128)(2,1)S(1)}, u32[]{:S(2)}, u32[]{:S(2)}) %all-to-all-start.3) | async-done | bytes 1572896 | tf_op jit(solution)/shard_map/all_to_all | solution.py:19
  102.5 5.0 %all-to-all-start.4 = ((bf16[4,64,3072]{2,1,0:T(8,128)(2,1)}), bf16[4,64,3072]{2,1,0:T(8,128)(2,1)S(1)}, u32[]{:S(2)}, u32[]{:S(2)}) async-start(bf16[4,64,3072]{2,1,0:T(8,128)(2,1)} %stack.22), calls=%async_computation.4 | async-start | bytes 3145728 | tf_op jit(solution)/shard_map/all_to_all | solution.py:19
  108.1 4.6 %convolution_multiply_fusion.2 = f32[256,1024]{1,0:T(8,128)S(1)} fusion(bf16[256,3072]{1,0:T(8,128)(2,1)S(1)} %bitcast.43, bf16[3072,1024]{1,0:T(8,128)(2,1)} %param.6, f32[]{:T(128)} %bitcast.11), kind=kOutput, calls=%fused_computation.2 | convolution fusion | flops 1610874880 | bytes 8912900 | tf_op jit(solution)/shard_map/dot_general | solution.py:17
  112.7 2.4 %add.17 = f32[256,1024]{1,0:T(8,128)} add(f32[256,1024]{1,0:T(8,128)} %collective-permute-done.2, f32[256,1024]{1,0:T(8,128)S(1)} %convolution_multiply_fusion.2) | non-fusion elementwise | flops 262144 | bytes 3145728 | tf_op jit(solution)/shard_map/add | solution.py:25
  115.1 8.4 %all-to-all-done.4 = bf16[4,64,3072]{2,1,0:T(8,128)(2,1)S(1)} async-done(((bf16[4,64,3072]{2,1,0:T(8,128)(2,1)}), bf16[4,64,3072]{2,1,0:T(8,128)(2,1)S(1)}, u32[]{:S(2)}, u32[]{:S(2)}) %all-to-all-start.4) | async-done | bytes 1572896 | tf_op jit(solution)/shard_map/all_to_all | solution.py:19
  124.9 5.0 %all-to-all-start.5 = ((bf16[4,64,3072]{2,1,0:T(8,128)(2,1)}), bf16[4,64,3072]{2,1,0:T(8,128)(2,1)S(1)}, u32[]{:S(2)}, u32[]{:S(2)}) async-start(bf16[4,64,3072]{2,1,0:T(8,128)(2,1)} %stack.23), calls=%async_computation.5 | async-start | bytes 3145728 | tf_op jit(solution)/shard_map/all_to_all | solution.py:19
  130.5 4.6 %convolution_multiply_fusion.1 = f32[256,1024]{1,0:T(8,128)S(1)} fusion(bf16[256,3072]{1,0:T(8,128)(2,1)S(1)} %bitcast.42, bf16[3072,1024]{1,0:T(8,128)(2,1)} %param.6, f32[]{:T(128)} %bitcast.14), kind=kOutput, calls=%fused_computation.1 | convolution fusion | flops 1610874880 | bytes 8912900 | tf_op jit(solution)/shard_map/dot_general | solution.py:17
  135.1 1.4 add.18
  137.4 7.4 %all-to-all-done.5 = bf16[4,64,3072]{2,1,0:T(8,128)(2,1)S(1)} async-done(((bf16[4,64,3072]{2,1,0:T(8,128)(2,1)}), bf16[4,64,3072]{2,1,0:T(8,128)(2,1)S(1)}, u32[]{:S(2)}, u32[]{:S(2)}) %all-to-all-start.5) | async-done | bytes 1572896 | tf_op jit(solution)/shard_map/all_to_all | solution.py:19
  144.8 4.6 %convolution_multiply_fusion = f32[256,1024]{1,0:T(8,128)S(1)} fusion(bf16[256,3072]{1,0:T(8,128)(2,1)S(1)} %bitcast.45, bf16[3072,1024]{1,0:T(8,128)(2,1)} %param.6, f32[]{:T(128)} %bitcast.17), kind=kOutput, calls=%fused_computation | convolution fusion | flops 1610874880 | bytes 8912900 | tf_op jit(solution)/shard_map/dot_general | solution.py:17
  149.3 5.0 %collective-permute-done.4 = f32[256,1024]{1,0:T(8,128)} collective-permute-done((f32[256,1024]{1,0:T(8,128)S(1)}, f32[256,1024]{1,0:T(8,128)}, u32[]{:S(2)}, u32[]{:S(2)}) %collective-permute-start.4) | collective-permute-done | bytes 1048608 | tf_op jit(solution)/shard_map/ppermute | solution.py:10
  155.8 17.5 %collective-permute-done.5 = f32[256,1024]{1,0:T(8,128)S(1)} collective-permute-done((f32[256,1024]{1,0:T(8,128)S(1)}, f32[256,1024]{1,0:T(8,128)S(1)}, u32[]{:S(2)}, u32[]{:S(2)}) %collective-permute-start.5) | collective-permute-done | bytes 1048608 | tf_op jit(solution)/shard_map/ppermute | solution.py:10
  (31 shorter events, 9.2 us)
Async XLA Ops:
  0.0 173.4 %copy-start = (bf16[1,256,256]{2,1,0:T(8,128)(2,1)S(1)}, bf16[1,256,256]{2,1,0:T(8,128)(2,1)}, u32[]{:S(2)}) copy-start(bf16[1,256,256]{2,1,0:T(8,128)(2,1)} %param.9) | copy-start | bytes 393220
  28.3 5.1 %copy-start.5 = (s32[1,6]{1,0:T(1,128)S(1)}, s32[1,6]{1,0:T(1,128)}, u32[]{:S(2)}) copy-start(s32[1,6]{1,0:T(1,128)} %param.8) | copy-start | bytes 76
  28.3 23.5 %all-to-all-start.1 = ((bf16[4,64,3072]{2,1,0:T(8,128)(2,1)}), bf16[4,64,3072]{2,1,0:T(8,128)(2,1)S(1)}, u32[]{:S(2)}, u32[]{:S(2)}) async-start(bf16[4,64,3072]{2,1,0:T(8,128)(2,1)} %stack.19), calls=%async_computation.1 | async-start | bytes 3145728 | tf_op jit(solution)/shard_map/all_to_all | solution.py:19
  40.3 19.4 %collective-permute-start = (f32[256,1024]{1,0:T(8,128)}, f32[256,1024]{1,0:T(8,128)}, u32[]{:S(2)}, u32[]{:S(2)}) collective-permute-start(f32[256,1024]{1,0:T(8,128)} %convolution_multiply_fusion.5), channel_id=1, source_target_pairs={{252,0},{0,4},{4,8},{8,12},{12,16},{16,20},{20,24},{24,28},{28,32}... | collective-permute-start | bytes 3145736 | tf_op jit(solution)/shard_map/ppermute | solution.py:10
  54.1 22.6 %all-to-all-start.2 = ((bf16[4,64,3072]{2,1,0:T(8,128)(2,1)}), bf16[4,64,3072]{2,1,0:T(8,128)(2,1)S(1)}, u32[]{:S(2)}, u32[]{:S(2)}) async-start(bf16[4,64,3072]{2,1,0:T(8,128)(2,1)} %stack.20), calls=%async_computation.2 | async-start | bytes 3145728 | tf_op jit(solution)/shard_map/all_to_all | solution.py:19
  65.5 24.6 %collective-permute-start.1 = (f32[256,1024]{1,0:T(8,128)}, f32[256,1024]{1,0:T(8,128)S(1)}, u32[]{:S(2)}, u32[]{:S(2)}) collective-permute-start(f32[256,1024]{1,0:T(8,128)} %fusion), channel_id=1, source_target_pairs={{252,0},{0,4},{4,8},{8,12},{12,16},{16,20},{20,24},{24,28},{28,32}... | collective-permute-start | bytes 3145736 | tf_op jit(solution)/shard_map/ppermute | solution.py:10
  76.8 2.6 %copy-start.1 = (bf16[4,64,3072]{2,1,0:T(8,128)(2,1)}, bf16[4,64,3072]{2,1,0:T(8,128)(2,1)S(1)}, u32[]{:S(2)}) copy-start(bf16[4,64,3072]{2,1,0:T(8,128)(2,1)S(1)} %all-to-all-done.2) | copy-start | bytes 4718596
  79.4 21.8 %all-to-all-start.3 = ((bf16[4,64,3072]{2,1,0:T(8,128)(2,1)}), bf16[4,64,3072]{2,1,0:T(8,128)(2,1)S(1)}, u32[]{:S(2)}, u32[]{:S(2)}) async-start(bf16[4,64,3072]{2,1,0:T(8,128)(2,1)} %stack.21), calls=%async_computation.3 | async-start | bytes 3145728 | tf_op jit(solution)/shard_map/all_to_all | solution.py:19
  90.1 11.1 %copy-start.3 = (bf16[64,3072]{1,0:T(8,128)(2,1)S(1)}, bf16[64,3072]{1,0:T(8,128)(2,1)}, u32[]{:S(2)}) copy-start(bf16[64,3072]{1,0:T(8,128)(2,1)} %get-tuple-element.10) | copy-start | bytes 1179652
  91.2 21.5 %collective-permute-start.2 = (f32[256,1024]{1,0:T(8,128)}, f32[256,1024]{1,0:T(8,128)}, u32[]{:S(2)}, u32[]{:S(2)}) collective-permute-start(f32[256,1024]{1,0:T(8,128)} %add.16), channel_id=1, source_target_pairs={{252,0},{0,4},{4,8},{8,12},{12,16},{16,20},{20,24},{24,28},{28,32}... | collective-permute-start | bytes 3145736 | tf_op jit(solution)/shard_map/ppermute | solution.py:10
  102.5 21.0 %all-to-all-start.4 = ((bf16[4,64,3072]{2,1,0:T(8,128)(2,1)}), bf16[4,64,3072]{2,1,0:T(8,128)(2,1)S(1)}, u32[]{:S(2)}, u32[]{:S(2)}) async-start(bf16[4,64,3072]{2,1,0:T(8,128)(2,1)} %stack.22), calls=%async_computation.4 | async-start | bytes 3145728 | tf_op jit(solution)/shard_map/all_to_all | solution.py:19
  112.7 10.8 %copy-start.2 = (bf16[64,3072]{1,0:T(8,128)(2,1)S(1)}, bf16[64,3072]{1,0:T(8,128)(2,1)}, u32[]{:S(2)}) copy-start(bf16[64,3072]{1,0:T(8,128)(2,1)} %get-tuple-element.5) | copy-start | bytes 1179652
  115.1 19.9 %collective-permute-start.3 = (f32[256,1024]{1,0:T(8,128)}, f32[256,1024]{1,0:T(8,128)}, u32[]{:S(2)}, u32[]{:S(2)}) collective-permute-start(f32[256,1024]{1,0:T(8,128)} %add.17), channel_id=1, source_target_pairs={{252,0},{0,4},{4,8},{8,12},{12,16},{16,20},{20,24},{24,28},{28,32}... | collective-permute-start | bytes 3145736 | tf_op jit(solution)/shard_map/ppermute | solution.py:10
  124.9 19.9 %all-to-all-start.5 = ((bf16[4,64,3072]{2,1,0:T(8,128)(2,1)}), bf16[4,64,3072]{2,1,0:T(8,128)(2,1)S(1)}, u32[]{:S(2)}, u32[]{:S(2)}) async-start(bf16[4,64,3072]{2,1,0:T(8,128)(2,1)} %stack.23), calls=%async_computation.5 | async-start | bytes 3145728 | tf_op jit(solution)/shard_map/all_to_all | solution.py:19
  136.5 17.9 %collective-permute-start.4 = (f32[256,1024]{1,0:T(8,128)S(1)}, f32[256,1024]{1,0:T(8,128)}, u32[]{:S(2)}, u32[]{:S(2)}) collective-permute-start(f32[256,1024]{1,0:T(8,128)S(1)} %add.18), channel_id=1, source_target_pairs={{252,0},{0,4},{4,8},{8,12},{12,16},{16,20},{20,24},{24,28},{28,32}... | collective-permute-start | bytes 3145736 | tf_op jit(solution)/shard_map/ppermute | solution.py:10
  149.3 24.0 %copy-start.4 = (bf16[256,1024]{1,0:T(8,128)(2,1)S(1)}, bf16[256,1024]{1,0:T(8,128)(2,1)}, u32[]{:S(2)}) copy-start(bf16[256,1024]{1,0:T(8,128)(2,1)} %param.5) | copy-start | bytes 1572868
  155.8 17.6 %collective-permute-start.5 = (f32[256,1024]{1,0:T(8,128)S(1)}, f32[256,1024]{1,0:T(8,128)S(1)}, u32[]{:S(2)}, u32[]{:S(2)}) collective-permute-start(f32[256,1024]{1,0:T(8,128)S(1)} %add.19), channel_id=1, source_target_pairs={{252,0},{0,4},{4,8},{8,12},{12,16},{16,20},{20,24},{24,28},{28,32}... | collective-permute-start | bytes 3145736 | tf_op jit(solution)/shard_map/ppermute | solution.py:10
